TPU v7x, 256 devices: a whole 4x4x8 slice. The times are simulated.
256 devices in a mesh: box: 16 (over x_lo, y, core), samp: 16 (over z, x_hi).
Axes of the slice: x: 4 (x_hi: 2, x_lo: 2; x = x_hi * 2 + x_lo), y: 4, z: 8, core: 2. Of those that a mesh axis runs over, the one named last changes fastest.
Arguments:
- xvec: bfloat16 [4096, 2, 4, 128], P(('box', 'samp')), may hold values from -6 to 6
- near_blocks: bfloat16 [4096, 8, 2, 128, 128], P(('box', 'samp')), may hold values from -0.1875 to 0.1875
- neighbours: int32 [4096, 8], P(('box', 'samp')), may hold values from 0 to 4095, as said below
- lift: bfloat16 [4096, 2, 128, 128], P(('box', 'samp')), may hold values from -0.5 to 0.5
- place: bfloat16 [4096, 2, 128, 128], P(('box', 'samp')), may hold values from -0.25 to 0.25
- interp: bfloat16 [2048, 128], replicated, may hold values from -0.5 to 0.5
- phases: float32 [8, 2, 2048], replicated, may hold values from -1 to 1, as said below
- octant: int32 [4096], P(('box', 'samp')), may hold values from 0 to 7, as said below
- leaf_parent_index: int32 [4096], P(('box', 'samp')), may hold values from 0 to 511, as said below
- translators: float32 [64, 2, 2048], P(None, None, 'samp'), may hold values from -0.5 to 0.5
- inter_list: int32 [512, 16], P('box'), may hold values from 0 to 511, as said below
- trans_id: int32 [512, 16], P('box'), may hold values from 0 to 63
Outputs:
- product: float32 [4096, 2, 4, 128], P(('box', 'samp'))
Inputs may be any that keep to these rules, and one draw needn't show every extreme that they name: `neighbours`: row n starts with n itself; its other entries are distinct and lie within 8 boxes of n in cyclic order over all 4096 leaf boxes (the texture is periodic). `leaf_parent_index`: leaf box n belongs to box group g = n // 256 and its parent is one of that group's upper-level boxes g * 32 to g * 32 + 31; every upper-level box has exactly 8 children. `octant`: the 8 children of an upper-level box have 8 distinct octants. `inter_list`: entries of row p are distinct, each equal to p + d modulo 512 with 2 <= |d| <= 32 (the periodic tree's interaction zone). `phases`: each entry has magnitude one: real part squared plus imaginary part squared is 1.
All inputs are finite; a program needn't handle non-finite values.
Results may differ from a plain program's by a relative error of at most 0.0065.
Values may be sent and summed in bfloat16 or wider, within the bound.
A program may use at most 64 MiB of HBM per device.

v0:
```python
import jax
import jax.numpy as jnp
from jax import lax
from jax.sharding import PartitionSpec as P


def with_halo(cells, sides, width):
    for axis, dim in sides:
        count = lax.axis_size(axis)
        head = lax.slice_in_dim(cells, 0, width, axis=dim)
        tail = lax.slice_in_dim(cells, cells.shape[dim] - width, cells.shape[dim], axis=dim)
        cells = jnp.concatenate(
            [
                lax.ppermute(tail, axis, [(i, (i + 1) % count) for i in range(count)]),
                cells,
                lax.ppermute(head, axis, [((i + 1) % count, i) for i in range(count)]),
            ],
            axis=dim,
        )
    return cells


def cmul(ar, ai, br, bi):
    return (ar * br - ai * bi, ar * bi + ai * br)


def on_device(
    xvec,
    near_blocks,
    neighbours,
    lift,
    place,
    interp,
    phases,
    octant,
    leaf_parent_index,
    translators,
    inter_list,
    trans_id,
):
    f32 = jnp.float32
    bf16 = jnp.bfloat16
    finest_precision = lax.Precision.HIGHEST
    boxes = xvec.shape[0]
    nsamp = lax.axis_size("samp")
    nboxaxis = lax.axis_size("box")
    box_index = lax.axis_index("box")
    samp_index = lax.axis_index("samp")
    compute_unit = box_index * nsamp + samp_index
    total = boxes * nsamp * nboxaxis
    reach = boxes // 2
    parents_here = boxes * nsamp // 8
    all_parents = parents_here * nboxaxis
    sample_share = interp.shape[0] // nsamp
    rhs_count = xvec.shape[2]
    widened = with_halo(xvec, ((("box", "samp"), 0),), reach)
    local_index = jnp.mod(neighbours - compute_unit * boxes + reach, total)
    near_x = jnp.take(widened, local_index, axis=0)

    def apply(a, b):
        return jnp.einsum("bkpq,bkrq->brp", a, b, preferred_element_type=f32)

    near_r = apply(near_blocks[:, :, 0], near_x[:, :, 0]) - apply(
        near_blocks[:, :, 1], near_x[:, :, 1]
    )
    near_i = apply(near_blocks[:, :, 0], near_x[:, :, 1]) + apply(
        near_blocks[:, :, 1], near_x[:, :, 0]
    )

    def radiate(a, b):
        return jnp.einsum("bqu,bru->brq", a, b, preferred_element_type=f32)

    pat_r = radiate(lift[:, 0], xvec[:, 0]) - radiate(lift[:, 1], xvec[:, 1])
    pat_i = radiate(lift[:, 0], xvec[:, 1]) + radiate(lift[:, 1], xvec[:, 0])
    pattern = jnp.stack([pat_r, pat_i], 1).astype(bf16)

    def phase_rows(octs):
        indicator_matrix = (octs[:, None] == jnp.arange(8, dtype=jnp.int32)[None, :]).astype(f32)
        return jnp.einsum("ex,xwf->ewf", indicator_matrix, phases, precision=finest_precision)

    def parent_table(pars):
        local = pars - box_index * parents_here
        return local[:, None] == jnp.arange(parents_here, dtype=jnp.int32)[None, :]

    rows_i = interp
    raised_terms = jnp.einsum("sq,bcrq->bcrs", rows_i, pattern, preferred_element_type=f32)
    shift = phase_rows(octant)
    cr, ci = cmul(
        shift[:, 0][:, None, :], shift[:, 1][:, None, :], raised_terms[:, 0], raised_terms[:, 1]
    )
    owner = parent_table(leaf_parent_index).astype(f32)
    sum_r = jnp.einsum("bp,brs->prs", owner, cr, precision=finest_precision)
    sum_i = jnp.einsum("bp,brs->prs", owner, ci, precision=finest_precision)
    term = jnp.stack([sum_r, sum_i], 1)
    term = term.reshape(parents_here, 2, rhs_count, 1 * lax.axis_size("samp"), sample_share)
    upward = lax.psum_scatter(
        jnp.transpose(term, (3, 0, 1, 2, 4)), "samp", scatter_dimension=0, tiled=True
    )[0]
    parent_pat = upward.astype(bf16)
    table_count = translators.shape[0]
    selector_index = (
        trans_id[:, :, None] == jnp.arange(table_count, dtype=jnp.int32)[None, None, :]
    ).astype(f32)
    operator_list = jnp.einsum(
        "yaw,wjt->yajt", selector_index, translators, precision=finest_precision
    )
    bordered = with_halo(parent_pat, (("box", 0),), parents_here)
    window_index = jnp.mod(inter_list - box_index * parents_here + parents_here, all_parents)
    select = (
        window_index[:, :, None] == jnp.arange(3 * parents_here, dtype=jnp.int32)[None, None, :]
    ).astype(bf16)
    fetched = jnp.einsum("pkj,jcrs->pkcrs", select, bordered, preferred_element_type=f32)
    tr_r = operator_list[:, :, 0][:, :, None, :]
    tr_i = operator_list[:, :, 1][:, :, None, :]
    add_r, add_i = cmul(tr_r, tr_i, fetched[:, :, 0], fetched[:, :, 1])
    incoming = jnp.stack([add_r.sum(1), add_i.sum(1)], 1).astype(bf16)
    owner = parent_table(leaf_parent_index).astype(bf16)
    chosen = jnp.einsum(
        "ei,ihfz->ehfz",
        owner,
        lax.all_gather(incoming, "samp", axis=3, tiled=True),
        preferred_element_type=f32,
    )
    shift = phase_rows(octant)
    sr, si = cmul(shift[:, 0][:, None, :], shift[:, 1][:, None, :], chosen[:, 0], chosen[:, 1])
    shifted = jnp.stack([sr, si], 1).astype(bf16)
    rows_i = interp
    field = jnp.einsum("bcrs,sq->bcrq", shifted, rows_i, preferred_element_type=f32)
    field = field.astype(bf16)

    def receive(a, b):
        return jnp.einsum("buq,brq->bru", a, b, preferred_element_type=f32)

    far_r = receive(place[:, 0], field[:, 0]) - receive(place[:, 1], field[:, 1])
    far_i = receive(place[:, 0], field[:, 1]) + receive(place[:, 1], field[:, 0])
    return jnp.stack([near_r + far_r, near_i + far_i], 1)


def solution(mesh):
    in_specs = (
        P(("box", "samp"), None, None, None),
        P(("box", "samp"), None, None, None, None),
        P(("box", "samp"), None),
        P(("box", "samp"), None, None, None),
        P(("box", "samp"), None, None, None),
        P(),
        P(),
        P(("box", "samp")),
        P(("box", "samp")),
        P(None, None, "samp"),
        P("box", None),
        P("box", None),
    )
    out_specs = P(("box", "samp"), None, None, None)
    return jax.shard_map(
        on_device, mesh=mesh, in_specs=in_specs, out_specs=out_specs, check_vma=False
    )
```

profile of v0, /device:TPU:2, one launch (start us, length us, event | category | flops | bytes accessed | tf_op | source)
XLA Modules:
  0.0 223.4 jit_solution(11524168463856257246)
XLA Ops:
  6.5 1.5 fusion.53
  8.0 1.4 fusion.55
  9.5 1.3 fusion.79
  10.8 1.4 fusion.36
  12.2 1.4 fusion.37
  13.7 0.3 fusion.58
  14.0 0.1 subtract_bitcast_fusion
  14.2 0.7 convolution_bitcast_fusion
  14.9 0.0 copy-start.8
  14.9 0.0 copy-start.2
  14.9 0.0 copy-start.4
  14.9 0.0 copy-start.3
  14.9 0.7 convolution_bitcast_fusion.1
  15.6 0.0 copy-start.5
  15.6 0.2 maximum_bitcast_fusion
  15.8 112.1 %all-reduce.2 = bf16[16,32,2,4,128]{4,1,0,3,2:T(8,128)(2,1)} all-reduce(f32[16,32,2,4,128]{4,1,0,3,2:T(8,128)S(1)} %maximum_bitcast_fusion), channel_id=2, replica_groups=mesh['box'=16,'samp'=16] {'samp'}, use_global_device_ids=true, to_apply=%region_0.1.clone | all-reduce | flops 524288 | bytes 3145728
  127.9 0.6 dynamic-slice
  128.5 1.5 fusion.83
  130.0 3.9 %collective-permute-start.3 = (bf16[32,2,4,128]{3,0,2,1:T(8,128)(2,1)S(1)}, bf16[32,2,4,128]{3,0,2,1:T(8,128)(2,1)S(1)}, u32[]{:S(2)}, u32[]{:S(2)}) collective-permute-start(bf16[32,2,4,128]{3,0,2,1:T(8,128)(2,1)S(1)} %fusion.83), channel_id=1, source_target_pairs={{16,0},{32,16},{48,32},{64,48},{80,64},{96,80},{112,96},{128,112},... | collective-permute-start | bytes 196616 | tf_op jit(solution)/shard_map/ppermute | solution.py:16
  133.9 1.4 collective-permute-start
  135.3 4.7 %collective-permute-start.1 = (bf16[8,2,4,128]{3,2,1,0:T(4,128)(2,1)S(1)}, bf16[8,2,4,128]{3,2,1,0:T(4,128)(2,1)S(1)}, u32[]{:S(2)}, u32[]{:S(2)}) collective-permute-start(bf16[8,2,4,128]{3,2,1,0:T(4,128)(2,1)S(1)} %get-tuple-element.20), channel_id=1, source_target_pairs={{1,0},{2,1},{3,2},{4,3},{5,4},{6,5},{7,6},{8,7},{9,8},{10,9},{11,1... | collective-permute-start | bytes 49160 | tf_op jit(solution)/shard_map/ppermute | solution.py:16
  139.9 0.1 copy.67
  140.0 0.4 fusion.69
  140.5 0.1 copy.69
  140.6 0.5 fusion.72
  141.1 0.7 subtract_reduce_fusion
  141.8 0.6 pad_maximum_fusion.1
  142.4 0.0 all-gather.2.cloned.1.call-update
  142.5 0.1 copy.62
  142.5 0.1 reshape.31
  142.6 0.1 copy.61
  142.7 0.1 pad_maximum_fusion
  142.8 0.8 gather_fusion
  143.6 0.1 copy.63
  143.7 0.2 broadcast_select_fusion
  144.0 3.4 %fusion.12 = f32[16,4,128]{2,1,0:T(4,128)S(1)} fusion(bf16[16,8,2,128,128]{4,3,2,1,0:T(8,128)(2,1)} %param.13, bf16[16,8,2,4,128]{4,3,1,0,2:T(4,128)(2,1)S(1)} %broadcast_select_fusion), kind=kOutput, calls=%fused_computation.17 | convolution fusion | flops 16777216 | bytes 4358144 | tf_op jit(solution)/shard_map/bkpq,bkrq->brp/dot_general | solution.py:61
  147.4 3.4 %fusion.15 = f32[16,4,128]{2,1,0:T(4,128)S(1)} fusion(bf16[16,8,2,128,128]{4,3,2,1,0:T(8,128)(2,1)} %param.13, bf16[16,8,2,4,128]{4,3,1,0,2:T(4,128)(2,1)S(1)} %broadcast_select_fusion), kind=kOutput, calls=%fused_computation.18 | convolution fusion | flops 16777216 | bytes 4358144 | tf_op jit(solution)/shard_map/bkpq,bkrq->brp/dot_general | solution.py:61
  150.8 3.4 %fusion.31 = f32[16,4,128]{2,1,0:T(4,128)S(1)} fusion(f32[16,4,128]{2,1,0:T(4,128)S(1)} %fusion.12, bf16[16,8,2,128,128]{4,3,2,1,0:T(8,128)(2,1)} %param.13, bf16[16,8,2,4,128]{4,3,1,0,2:T(4,128)(2,1)S(1)} %broadcast_select_fusion), kind=kOutput, calls=%fused_computation.30 | convolution fusion | flops 16785408 | bytes 4390912 | tf_op jit(solution)/shard_map/bkpq,bkrq->brp/dot_general | solution.py:61
  154.2 3.5 %fusion.28 = f32[16,4,128]{2,1,0:T(4,128)S(1)} fusion(f32[16,4,128]{2,1,0:T(4,128)S(1)} %fusion.15, bf16[16,8,2,128,128]{4,3,2,1,0:T(8,128)(2,1)} %param.13, bf16[16,8,2,4,128]{4,3,1,0,2:T(4,128)(2,1)S(1)} %broadcast_select_fusion), kind=kOutput, calls=%fused_computation.29 | convolution fusion | flops 16785408 | bytes 4390912 | tf_op jit(solution)/shard_map/bkpq,bkrq->brp/dot_general | solution.py:61
  157.7 54.6 %all-gather.2.cloned.1.call-done = bf16[32,2,4,2048]{3,0,2,1:T(8,128)(2,1)} async-done(((bf16[32,2,4,128]{3,0,2,1:T(8,128)(2,1)}), bf16[32,2,4,2048]{3,0,2,1:T(8,128)(2,1)}) %all-gather.2.cloned.1.call-update) | async-done | bytes 1048592 | tf_op jit(solution)/shard_map/all_gather | solution.py:121
  212.3 1.6 fusion.103
  213.8 0.1 subtract_convert_fusion
  214.0 0.3 convolution_convert_fusion
  214.3 0.4 fusion.49
  214.7 0.4 fusion.47
  215.1 0.4 fusion.27
  215.4 0.4 fusion.25
  215.9 0.6 copy.87
  (30 shorter events, 0.3 us)
Async XLA Ops:
  6.5 7.2 %copy-start = (bf16[2048,128]{1,0:T(8,128)(2,1)S(1)}, bf16[2048,128]{1,0:T(8,128)(2,1)}, u32[]{:S(2)}) copy-start(bf16[2048,128]{1,0:T(8,128)(2,1)} %param.17) | copy-start | bytes 1572868
  6.5 7.5 %copy-start.7 = (s32[16]{0:T(128)S(1)}, s32[16]{0:T(128)}, u32[]{:S(2)}) copy-start(s32[16]{0:T(128)} %param.20) | copy-start | bytes 196
  6.5 205.7 %all-gather.2.cloned.1.call-start = ((), (), s32[]{:S(2)}) async-start(), calls=%async_computation | async-start | bytes 1114112 | tf_op jit(solution)/shard_map/all_gather | solution.py:121
  14.9 113.1 %copy-start.8 = (u32[256]{0:T(256)S(1)}, u32[256]{0:T(256)}, u32[]{:S(2)}) copy-start(u32[256]{0:T(256)} %constant.68) | copy-start | bytes 3076
  14.9 119.0 %copy-start.2 = (bf16[16,2,4,128]{3,2,1,0:T(4,128)(2,1)S(1)}, bf16[16,2,4,128]{3,2,1,0:T(4,128)(2,1)}, u32[]{:S(2)}) copy-start(bf16[16,2,4,128]{3,2,1,0:T(4,128)(2,1)} %param.12) | copy-start | bytes 98308
  14.9 125.0 %copy-start.4 = (s32[32,16]{0,1:T(8,128)S(1)}, s32[32,16]{0,1:T(8,128)}, u32[]{:S(2)}) copy-start(s32[32,16]{0,1:T(8,128)} %param.23) | copy-start | bytes 6148
  14.9 125.1 %copy-start.3 = (f32[64,2,128]{2,1,0:T(2,128)S(1)}, f32[64,2,128]{2,1,0:T(2,128)}, u32[]{:S(2)}) copy-start(f32[64,2,128]{2,1,0:T(2,128)} %param.21) | copy-start | bytes 196612
  15.6 124.9 %copy-start.5 = (s32[32,16]{0,1:T(8,128)S(1)}, s32[32,16]{0,1:T(8,128)}, u32[]{:S(2)}) copy-start(s32[32,16]{0,1:T(8,128)} %param.22) | copy-start | bytes 6148
  127.9 14.5 %copy-start.6 = (s32[16,8]{0,1:T(8,128)S(1)}, s32[16,8]{0,1:T(8,128)}, u32[]{:S(2)}) copy-start(s32[16,8]{0,1:T(8,128)} %param.14) | copy-start | bytes 1540
  130.0 10.6 %collective-permute-start.2 = (bf16[32,2,4,128]{3,0,2,1:T(8,128)(2,1)S(1)}, bf16[32,2,4,128]{3,0,2,1:T(8,128)(2,1)S(1)}, u32[]{:S(2)}, u32[]{:S(2)}) collective-permute-start(bf16[32,2,4,128]{3,0,2,1:T(8,128)(2,1)S(1)} %fusion.83), channel_id=1, source_target_pairs={{0,16},{16,32},{32,48},{48,64},{64,80},{80,96},{96,112},{112,128},... | collective-permute-start | bytes 196616 | tf_op jit(solution)/shard_map/ppermute | solution.py:14
  130.0 10.6 %collective-permute-start.3 = (bf16[32,2,4,128]{3,0,2,1:T(8,128)(2,1)S(1)}, bf16[32,2,4,128]{3,0,2,1:T(8,128)(2,1)S(1)}, u32[]{:S(2)}, u32[]{:S(2)}) collective-permute-start(bf16[32,2,4,128]{3,0,2,1:T(8,128)(2,1)S(1)} %fusion.83), channel_id=1, source_target_pairs={{16,0},{32,16},{48,32},{64,48},{80,64},{96,80},{112,96},{128,112},... | collective-permute-start | bytes 196616 | tf_op jit(solution)/shard_map/ppermute | solution.py:16
  133.9 8.9 %collective-permute-start = (bf16[8,2,4,128]{3,2,1,0:T(4,128)(2,1)S(1)}, bf16[8,2,4,128]{3,2,1,0:T(4,128)(2,1)S(1)}, u32[]{:S(2)}, u32[]{:S(2)}) collective-permute-start(bf16[8,2,4,128]{3,2,1,0:T(4,128)(2,1)S(1)} %get-tuple-element.19), channel_id=1, source_target_pairs={{0,1},{1,2},{2,3},{3,4},{4,5},{5,6},{6,7},{7,8},{8,9},{9,10},{10,1... | collective-permute-start | bytes 49160 | tf_op jit(solution)/shard_map/ppermute | solution.py:14
  135.3 7.5 %collective-permute-start.1 = (bf16[8,2,4,128]{3,2,1,0:T(4,128)(2,1)S(1)}, bf16[8,2,4,128]{3,2,1,0:T(4,128)(2,1)S(1)}, u32[]{:S(2)}, u32[]{:S(2)}) collective-permute-start(bf16[8,2,4,128]{3,2,1,0:T(4,128)(2,1)S(1)} %get-tuple-element.20), channel_id=1, source_target_pairs={{1,0},{2,1},{3,2},{4,3},{5,4},{6,5},{7,6},{8,7},{9,8},{10,9},{11,1... | collective-permute-start | bytes 49160 | tf_op jit(solution)/shard_map/ppermute | solution.py:16
  154.2 60.1 %copy-start.1 = (bf16[16,2,128,128]{3,2,1,0:T(8,128)(2,1)S(1)}, bf16[16,2,128,128]{3,2,1,0:T(8,128)(2,1)}, u32[]{:S(2)}) copy-start(bf16[16,2,128,128]{3,2,1,0:T(8,128)(2,1)} %param.16) | copy-start | bytes 3145732
Sparse Core Ops, SparseCore 0:
  142.6 69.6 all-gather.1
where the time goes:
time: 225 us; the launch traced here: 223 us
  blocking collectives  112 us (50%)
  waiting for transfers between devices  54.6 us (24%)
  matrix products  26.8 us (12%)
  between operations  13.7 us (6%)
  starting transfers between devices  9.91 us (4%)
  local copies, waits for them, and re-layouts  4.17 us (2%)
    unnamed x1, blocking collectives  112 us
    all_gather x1, waiting for transfers between devices, on_device(): lax.all_gather(incoming, 'samp', axis=3, tiled=True)  54.6 us
    dot_general x4, matrix products, apply(): return jnp.einsum('bkpq,bkrq->brp', a, b, preferred_element_type=f32)  13.7 us
    ppermute x2, starting transfers between devices, with_halo(): lax.ppermute(head, axis, [((i + 1) % count, i) for i in range(count)])  8.5 us
    dot_general x4, matrix products, radiate(): return jnp.einsum('bqu,bru->brq', a, b, preferred_element_type=f32)  5.78 us
  transfers between devices with their start and end apart: 5, of which 1 were waited for; matrix products, arithmetic and copies ran while one was open for 8% of the time, Pallas kernels for 0%

commit v1 on v0

v1 whole, which is shorter than its diff:
```python
import jax
import jax.numpy as jnp
from jax import lax
from jax.experimental import pallas as pl
from jax.experimental.pallas import tpu as pltpu
from jax.sharding import PartitionSpec as P

f32 = jnp.float32
bf16 = jnp.bfloat16
MESH = pl.DeviceIdType.MESH
NT_DIMS = (((1,), (1,)), ((), ()))


def dot_nt(a, b):
    return lax.dot_general(a, b, NT_DIMS, preferred_element_type=f32)


def dot_nn(a, b):
    return jnp.dot(a, b, preferred_element_type=f32)


def times_i(v):
    swapped = pltpu.roll(v, 4, 0)
    row = lax.broadcasted_iota(jnp.int32, v.shape, 0)
    return jnp.where(row < 4, -swapped, swapped)


def make_kernel(nbox, nsamp, boxes, parents, near_k, list_k, sample_share):
    half = boxes // 2
    total_boxes = boxes * nsamp * nbox
    total_parents = parents * nbox
    blk = boxes * 8
    pb = parents * 8
    slots = boxes * nsamp
    share = sample_share

    def kernel(
        nbr, octs, pars, ilist, tids,
        x_hbm, near_hbm, lift_hbm, place_hbm, interp_hbm, phases_hbm, trans_hbm,
        out,
        xh, xf, nearm, liftm, placem, interpm, phm, trm,
        patf, slotf, gbuf, parf, parw, parb, hbuf, incf, sbuf, rbuf, nearf, fieldf,
        near_sem, in_sem,
        halo_send, halo_recv, g_send, g_recv, h_send, h_recv, a_send, a_recv,
    ):
        b = lax.axis_index("box")
        s = lax.axis_index("samp")
        me = b * nsamp + s
        ndev = nbox * nsamp

        x_cp = pltpu.make_async_copy(x_hbm, xh.at[pl.ds(half * 8, blk)], in_sem.at[0])
        lift_cp = pltpu.make_async_copy(lift_hbm, liftm, in_sem.at[1])
        interp_cp = pltpu.make_async_copy(interp_hbm, interpm, in_sem.at[2])
        ph_cp = pltpu.make_async_copy(
            phases_hbm.at[:, :, pl.ds(pl.multiple_of(s * share, share), share)], phm, in_sem.at[3]
        )
        tr_cp = pltpu.make_async_copy(trans_hbm, trm, in_sem.at[4])
        place_cp = pltpu.make_async_copy(place_hbm, placem, in_sem.at[5])
        near_cps = [
            pltpu.make_async_copy(near_hbm.at[n], nearm.at[n], near_sem.at[n]) for n in range(boxes)
        ]
        x_cp.start()
        lift_cp.start()

        barrier = pltpu.get_barrier_semaphore()
        right = lax.rem(me + 1, ndev)
        left = lax.rem(me + ndev - 1, ndev)
        right_id = (right // nsamp, lax.rem(right, nsamp))
        left_id = (left // nsamp, lax.rem(left, nsamp))
        up_id = (lax.rem(b + 1, nbox), s)
        down_id = (lax.rem(b + nbox - 1, nbox), s)

        def peer(t):
            return (b, lax.rem(s + t + nsamp, nsamp))

        for dev in (right_id, left_id, up_id, down_id):
            pl.semaphore_signal(barrier, inc=1, device_id=dev, device_id_type=MESH)
        for t in range(1, nsamp):
            pl.semaphore_signal(barrier, inc=1, device_id=peer(t), device_id_type=MESH)

        interp_cp.start()
        ph_cp.start()
        tr_cp.start()
        for cp in near_cps[: boxes // 2]:
            cp.start()
        place_cp.start()
        for cp in near_cps[boxes // 2 :]:
            cp.start()

        for n in range(boxes):
            slot = octs[n] * parents + (pars[n] - b * parents)
            slotf[pl.ds(n, 1), :] = jnp.full((1, 128), slot, jnp.int32).astype(f32)
        x_cp.wait()
        xf[pl.ds(half, boxes)] = xh[pl.ds(half * 8, blk), :].astype(f32).reshape(boxes, 8, 128)
        lift_cp.wait()

        for n in range(boxes):
            xn = xf[half + n].astype(bf16)
            o = dot_nt(xn, liftm[n].reshape(2 * liftm.shape[2], liftm.shape[3]))
            patf[pl.ds(n, 8, stride=boxes), :] = o[:, :128] + times_i(o[:, 128:])
        gbuf[0, pl.ds(0, blk), :] = patf[...].astype(bf16)
        gbuf[0, pl.ds(blk, boxes), :] = slotf[...].astype(bf16)

        pl.semaphore_wait(barrier, nsamp - 1 + 4)

        to_right = pltpu.make_async_remote_copy(
            src_ref=xh.at[pl.ds(blk, half * 8)], dst_ref=xh.at[pl.ds(0, half * 8)],
            send_sem=halo_send.at[0], recv_sem=halo_recv.at[0],
            device_id=right_id, device_id_type=MESH,
        )
        to_left = pltpu.make_async_remote_copy(
            src_ref=xh.at[pl.ds(half * 8, half * 8)], dst_ref=xh.at[pl.ds(blk + half * 8, half * 8)],
            send_sem=halo_send.at[1], recv_sem=halo_recv.at[1],
            device_id=left_id, device_id_type=MESH,
        )
        to_right.start()
        to_left.start()
        order = sorted(range(1, nsamp), key=lambda t: -min(t, nsamp - t))
        gathers = {
            t: pltpu.make_async_remote_copy(
                src_ref=gbuf.at[0], dst_ref=gbuf.at[t],
                send_sem=g_send.at[t], recv_sem=g_recv.at[t],
                device_id=peer(t), device_id_type=MESH,
            )
            for t in range(1, nsamp)
        }
        for t in order:
            gathers[t].start()

        to_right.wait()
        to_left.wait()
        xf[pl.ds(0, half)] = xh[pl.ds(0, half * 8), :].astype(f32).reshape(half, 8, 128)
        xf[pl.ds(half + boxes, half)] = (
            xh[pl.ds(blk + half * 8, half * 8), :].astype(f32).reshape(half, 8, 128)
        )

        def near_box(n, carry):
            pltpu.make_async_copy(near_hbm.at[n], nearm.at[n], near_sem.at[n]).wait()
            acc = jnp.zeros((8, 256), f32)
            for k in range(near_k):
                idx = lax.rem(nbr[n, k] - me * boxes + half + total_boxes, 2 * boxes)
                xk = xf[idx].astype(bf16)
                acc = acc + dot_nt(xk, nearm[n, k].reshape(256, 128))
            nearf[pl.ds(pl.multiple_of(n * 8, 8), 8), :] = acc[:, :128] + times_i(acc[:, 128:])
            return carry

        lax.fori_loop(0, boxes // 2, near_box, 0)

        interp_cp.wait()
        ph_cp.wait()
        tr_cp.wait()
        for t in range(1, nsamp):
            gathers[t].wait()

        ids = gbuf[:, pl.ds(blk, boxes), :].reshape(slots, 128).astype(f32)
        lane = lax.broadcasted_iota(jnp.int32, (slots, 128), 1).astype(f32)
        spread = jnp.concatenate(
            [jnp.where(ids == lane + 128.0 * h, 1.0, 0.0) for h in range(slots // 128)], axis=1
        ).astype(bf16)
        ids_t = ids.T
        row = lax.broadcasted_iota(jnp.int32, (128, slots), 0).astype(f32)
        gather_m = jnp.concatenate(
            [jnp.where(ids_t == row + 128.0 * h, 1.0, 0.0) for h in range(slots // 128)], axis=0
        ).astype(bf16)
        interp_own = interpm[pl.ds(pl.multiple_of(s * share, share), share), :]

        def raised(cr):
            sorted_pat = dot_nn(
                gather_m, gbuf[:, pl.ds(cr * boxes, boxes), :].reshape(slots, 128)
            ).astype(bf16)
            return dot_nt(sorted_pat, interp_own)

        for r in range(4):
            ar, ai = raised(r), raised(4 + r)
            pr = jnp.zeros((parents, 128), f32)
            pi = jnp.zeros((parents, 128), f32)
            for o in range(8):
                fr, fi = phm[o, pl.ds(0, 1), :], phm[o, pl.ds(1, 1), :]
                br, bi = ar[o * parents : (o + 1) * parents], ai[o * parents : (o + 1) * parents]
                pr = pr + (fr * br - fi * bi)
                pi = pi + (fr * bi + fi * br)
            parf[pl.ds(r, parents, stride=8), :] = pr
            parf[pl.ds(4 + r, parents, stride=8), :] = pi
        parb[...] = parf[...].astype(bf16)

        to_up = pltpu.make_async_remote_copy(
            src_ref=parb, dst_ref=hbuf.at[0], send_sem=h_send.at[0], recv_sem=h_recv.at[0],
            device_id=up_id, device_id_type=MESH,
        )
        to_down = pltpu.make_async_remote_copy(
            src_ref=parb, dst_ref=hbuf.at[1], send_sem=h_send.at[1], recv_sem=h_recv.at[1],
            device_id=down_id, device_id_type=MESH,
        )
        to_up.start()
        to_down.start()
        parw[pl.ds(parents, parents)] = parb[...].astype(f32).reshape(parents, 8, 128)
        to_up.wait()
        parw[pl.ds(0, parents)] = hbuf[0].astype(f32).reshape(parents, 8, 128)
        to_down.wait()
        parw[pl.ds(2 * parents, parents)] = hbuf[1].astype(f32).reshape(parents, 8, 128)

        def translate(p, carry):
            s1 = jnp.zeros((8, 128), f32)
            s2 = jnp.zeros((8, 128), f32)
            for k in range(list_k):
                w = lax.rem(ilist[p, k] - b * parents + parents + total_parents, total_parents)
                v = parw[jnp.minimum(w, 3 * parents - 1)]
                op = trm[tids[p, k]]
                s1 = s1 + op[0:1] * v
                s2 = s2 + op[1:2] * v
            inc = (s1 + times_i(s2)).astype(bf16).astype(f32)
            incf[pl.ds(pl.multiple_of(p * 8, 8), 8), :] = inc
            return carry

        lax.fori_loop(0, parents, translate, 0)

        for r in range(4):
            ir = incf[pl.ds(r, parents, stride=8), :]
            ii = incf[pl.ds(4 + r, parents, stride=8), :]
            sr, si = [], []
            for o in range(8):
                fr, fi = phm[o, pl.ds(0, 1), :], phm[o, pl.ds(1, 1), :]
                sr.append((fr * ir - fi * ii).astype(bf16))
                si.append((fr * ii + fi * ir).astype(bf16))
            for cr, part in ((r, sr), (4 + r, si)):
                u = dot_nn(spread, jnp.concatenate(part, axis=0)).astype(bf16)
                sbuf[:, pl.ds(cr * boxes, boxes), :] = u.reshape(nsamp, boxes, 128)

        sends = {
            t: pltpu.make_async_remote_copy(
                src_ref=sbuf.at[t], dst_ref=rbuf.at[t],
                send_sem=a_send.at[t], recv_sem=a_recv.at[t],
                device_id=peer(-t), device_id_type=MESH,
            )
            for t in range(1, nsamp)
        }
        for t in order:
            sends[t].start()

        lax.fori_loop(boxes // 2, boxes, near_box, 0)

        def lowered(t, block):
            j = lax.rem(s + t, nsamp)
            return dot_nn(block, interpm[pl.ds(pl.multiple_of(j * share, share), share), :])

        field = lowered(0, sbuf[0])
        for t in sorted(range(1, nsamp), key=lambda t: min(t, nsamp - t)):
            sends[t].wait()
            field = field + lowered(t, rbuf[t])
        fieldf[...] = field
        place_cp.wait()
        for n in range(boxes):
            fn = fieldf[pl.ds(n, 8, stride=boxes), :].astype(bf16)
            o = dot_nt(fn, placem[n].reshape(256, 128))
            out[pl.ds(n * 8, 8), :] = nearf[pl.ds(n * 8, 8), :] + o[:, :128] + times_i(o[:, 128:])

    return kernel


def on_device(
    xvec, near_blocks, neighbours, lift, place, interp, phases, octant,
    leaf_parent_index, translators, inter_list, trans_id,
):
    boxes = xvec.shape[0]
    nsamp = lax.axis_size("samp")
    nbox = lax.axis_size("box")
    parents = inter_list.shape[0]
    share = interp.shape[0] // nsamp
    blk = boxes * 8
    x2 = xvec.reshape(blk, 128)
    smem = pl.BlockSpec(memory_space=pltpu.SMEM)
    hbm = pl.BlockSpec(memory_space=pltpu.HBM)
    dma = pltpu.SemaphoreType.DMA
    out = pl.pallas_call(
        make_kernel(nbox, nsamp, boxes, parents, neighbours.shape[1], inter_list.shape[1], share),
        out_shape=jax.ShapeDtypeStruct((blk, 128), f32),
        in_specs=[smem] * 5 + [hbm] * 7,
        out_specs=pl.BlockSpec(memory_space=pltpu.VMEM),
        scratch_shapes=[
            pltpu.VMEM((2 * blk, 128), bf16),
            pltpu.VMEM((2 * boxes, 8, 128), f32),
            pltpu.VMEM(near_blocks.shape, bf16),
            pltpu.VMEM(lift.shape, bf16),
            pltpu.VMEM(place.shape, bf16),
            pltpu.VMEM(interp.shape, bf16),
            pltpu.VMEM((8, 2, share), f32),
            pltpu.VMEM(translators.shape, f32),
            pltpu.VMEM((blk, 128), f32),
            pltpu.VMEM((boxes, 128), f32),
            pltpu.VMEM((nsamp, blk + boxes, 128), bf16),
            pltpu.VMEM((parents * 8, 128), f32),
            pltpu.VMEM((3 * parents, 8, 128), f32),
            pltpu.VMEM((parents * 8, 128), bf16),
            pltpu.VMEM((2, parents * 8, 128), bf16),
            pltpu.VMEM((parents * 8, 128), f32),
            pltpu.VMEM((nsamp, blk, 128), bf16),
            pltpu.VMEM((nsamp, blk, 128), bf16),
            pltpu.VMEM((blk, 128), f32),
            pltpu.VMEM((blk, 128), f32),
            dma((boxes,)),
            dma((6,)),
            dma((2,)), dma((2,)),
            dma((nsamp,)), dma((nsamp,)),
            dma((2,)), dma((2,)),
            dma((nsamp,)), dma((nsamp,)),
        ],
        compiler_params=pltpu.CompilerParams(
            collective_id=0, has_side_effects=True, vmem_limit_bytes=60 * 1024 * 1024
        ),
    )(
        neighbours, octant, leaf_parent_index, inter_list, trans_id,
        x2, near_blocks, lift, place, interp, phases, translators,
    )
    return out.reshape(xvec.shape)


def solution(mesh):
    lead = ("box", "samp")
    in_specs = (
        P(lead, None, None, None),
        P(lead, None, None, None, None),
        P(lead, None),
        P(lead, None, None, None),
        P(lead, None, None, None),
        P(),
        P(),
        P(lead),
        P(lead),
        P(None, None, "samp"),
        P("box", None),
        P("box", None),
    )
    return jax.shard_map(
        on_device, mesh=mesh, in_specs=in_specs, out_specs=P(lead, None, None, None), check_vma=False
    )
```

time: 225 us -> 58.8 us (0.26)
  the two profiles are of different devices: /device:TPU:2 before, /device:TPU:1 now
where the time goes in v1:
time: 58.8 us; the launch traced here: 58.5 us
  Pallas kernels  52.9 us (90%)
  local copies, waits for them, and re-layouts  5.57 us (9%)
    pallas_call x1, Pallas kernels, on_device(): pl.pallas_call(make_kernel(nbox, nsamp, boxes, parents, neighbours.shape[...  52.9 us
    unnamed x4, local copies, waits for them, and re-layouts  5.57 us

profile of v1, /device:TPU:1, one launch (start us, length us, event | category | flops | bytes accessed | tf_op | source)
XLA Modules:
  0.0 58.5 jit_solution(5833040232901007847)
XLA Ops:
  0.0 1.4 %copy.13.nbr = s32[16,8]{1,0:T(8,128)} copy(s32[16,8]{0,1:T(8,128)} %param.14) | data formatting | bytes 1024 | tf_op args[2]
  1.4 1.4 %copy.14.ilist = s32[32,16]{1,0:T(8,128)} copy(s32[32,16]{0,1:T(8,128)} %param.22) | data formatting | bytes 4096 | tf_op args[10]
  2.7 1.4 %copy.15.tids = s32[32,16]{1,0:T(8,128)} copy(s32[32,16]{0,1:T(8,128)} %param.23) | data formatting | bytes 4096 | tf_op args[11]
  4.1 52.9 %shard_map.118 = f32[128,128]{1,0:T(8,128)} custom-call(s32[16,8]{1,0:T(8,128)} %copy.13.nbr, s32[16]{0:T(128)} %octs.1, s32[16]{0:T(128)} %pars.1, s32[32,16]{1,0:T(8,128)} %copy.14.ilist, s32[32,16]{1,0:T(8,128)} %copy.15.tids, bf16[128,128]{1,0:T(8,128)(2,1)} %bitcast.3, bf16[16,8,2,128,128]{4,3,2,1,0:T(8,128)(2,1)} %near_hbm.1, ...), custom_call_target="tpu_custom_call" | custom-call | tf_op jit(solution)/shard_map/pallas_call | solution.py:274
  57.0 1.5 %copy.17 = f32[16,2,4,128]{3,2,1,0:T(4,128)} copy(f32[16,2,4,128]{3,2,1,0:T(4,128)} %bitcast.2) | data formatting | bytes 131072

commit v2 on v1

--- a/solution.py
+++ b/solution.py
@@ -32,16 +32,19 @@
     blk = boxes * 8
     pb = parents * 8
     slots = boxes * nsamp
+    nz = nsamp // 2
     share = sample_share
 
     def kernel(
         nbr, octs, pars, ilist, tids,
         x_hbm, near_hbm, lift_hbm, place_hbm, interp_hbm, phases_hbm, trans_hbm,
         out,
-        xh, xf, nearm, liftm, placem, interpm, phm, trm,
-        patf, slotf, gbuf, parf, parw, parb, hbuf, incf, sbuf, rbuf, nearf, fieldf,
+        xh, xf, nearm, liftm, placem, interpm, phm, trm, trb,
+        patf, slotf, gbuf, parf, parw, parb, hbuf, incf,
+        ownf, xsend, xrecv, zsend, zrecv, nearf, fieldf,
         near_sem, in_sem,
-        halo_send, halo_recv, g_send, g_recv, h_send, h_recv, a_send, a_recv,
+        halo_send, halo_recv, g_send, g_recv, h_send, h_recv,
+        ax_send, ax_recv, az_send, az_recv,
     ):
         b = lax.axis_index("box")
         s = lax.axis_index("samp")
@@ -50,7 +53,9 @@
 
         x_cp = pltpu.make_async_copy(x_hbm, xh.at[pl.ds(half * 8, blk)], in_sem.at[0])
         lift_cp = pltpu.make_async_copy(lift_hbm, liftm, in_sem.at[1])
-        interp_cp = pltpu.make_async_copy(interp_hbm, interpm, in_sem.at[2])
+        interp_cp = pltpu.make_async_copy(
+            interp_hbm.at[pl.ds(pl.multiple_of(s * share, share), share)], interpm, in_sem.at[2]
+        )
         ph_cp = pltpu.make_async_copy(
             phases_hbm.at[:, :, pl.ds(pl.multiple_of(s * share, share), share)], phm, in_sem.at[3]
         )
@@ -70,13 +75,16 @@
         up_id = (lax.rem(b + 1, nbox), s)
         down_id = (lax.rem(b + nbox - 1, nbox), s)
 
-        def peer(t):
-            return (b, lax.rem(s + t + nsamp, nsamp))
-
-        for dev in (right_id, left_id, up_id, down_id):
+        z, xhi = s // 2, lax.rem(s, 2)
+        partner = (b, s + 1 - 2 * xhi)
+
+        def along(t):
+            return (b, 2 * lax.rem(z + t + nz, nz) + xhi)
+
+        for dev in (right_id, left_id, up_id, down_id, partner):
             pl.semaphore_signal(barrier, inc=1, device_id=dev, device_id_type=MESH)
-        for t in range(1, nsamp):
-            pl.semaphore_signal(barrier, inc=1, device_id=peer(t), device_id_type=MESH)
+        for t in range(1, nz):
+            pl.semaphore_signal(barrier, inc=1, device_id=along(t), device_id_type=MESH)
 
         interp_cp.start()
         ph_cp.start()
@@ -101,7 +109,7 @@
         gbuf[0, pl.ds(0, blk), :] = patf[...].astype(bf16)
         gbuf[0, pl.ds(blk, boxes), :] = slotf[...].astype(bf16)
 
-        pl.semaphore_wait(barrier, nsamp - 1 + 4)
+        pl.semaphore_wait(barrier, nz - 1 + 5)
 
         to_right = pltpu.make_async_remote_copy(
             src_ref=xh.at[pl.ds(blk, half * 8)], dst_ref=xh.at[pl.ds(0, half * 8)],
@@ -115,17 +123,27 @@
         )
         to_right.start()
         to_left.start()
-        order = sorted(range(1, nsamp), key=lambda t: -min(t, nsamp - t))
-        gathers = {
-            t: pltpu.make_async_remote_copy(
+        order = sorted(range(1, nz), key=lambda t: -min(t, nz - t))
+
+        def spread_out(t):
+            return pltpu.make_async_remote_copy(
                 src_ref=gbuf.at[0], dst_ref=gbuf.at[t],
                 send_sem=g_send.at[t], recv_sem=g_recv.at[t],
-                device_id=peer(t), device_id_type=MESH,
-            )
-            for t in range(1, nsamp)
-        }
+                device_id=along(t), device_id_type=MESH,
+            )
+
+        def hand_over(t):
+            return pltpu.make_async_remote_copy(
+                src_ref=gbuf.at[t], dst_ref=gbuf.at[nz + t],
+                send_sem=g_send.at[nz + t], recv_sem=g_recv.at[nz + t],
+                device_id=partner, device_id_type=MESH,
+            )
+
+        gathers = {t: spread_out(t) for t in order}
+        gathers.update({nz + t: hand_over(t) for t in range(nz)})
         for t in order:
             gathers[t].start()
+        gathers[nz].start()
 
         to_right.wait()
         to_left.wait()
@@ -138,19 +156,35 @@
             pltpu.make_async_copy(near_hbm.at[n], nearm.at[n], near_sem.at[n]).wait()
             acc = jnp.zeros((8, 256), f32)
             for k in range(near_k):
-                idx = lax.rem(nbr[n, k] - me * boxes + half + total_boxes, 2 * boxes)
+                idx = lax.rem(nbr[k, n] - me * boxes + half + total_boxes, 2 * boxes)
                 xk = xf[idx].astype(bf16)
                 acc = acc + dot_nt(xk, nearm[n, k].reshape(256, 128))
             nearf[pl.ds(pl.multiple_of(n * 8, 8), 8), :] = acc[:, :128] + times_i(acc[:, 128:])
             return carry
 
-        lax.fori_loop(0, boxes // 2, near_box, 0)
+        done = 0
+        for i, t in enumerate(order):
+            upto = boxes * (i + 1) // (2 * len(order))
+            lax.fori_loop(done, upto, near_box, 0)
+            done = upto
+            gathers[t].wait_recv()
+            gathers[nz + t].start()
 
         interp_cp.wait()
         ph_cp.wait()
         tr_cp.wait()
-        for t in range(1, nsamp):
-            gathers[t].wait()
+
+        def widen(t, carry):
+            op = trm[t]
+            trb[2 * t] = jnp.broadcast_to(op[0:1], (8, 128))
+            trb[2 * t + 1] = jnp.broadcast_to(op[1:2], (8, 128))
+            return carry
+
+        lax.fori_loop(0, trm.shape[0], widen, 0, unroll=8)
+        for t in order:
+            gathers[t].wait_send()
+        for t in range(nz):
+            gathers[nz + t].wait()
 
         ids = gbuf[:, pl.ds(blk, boxes), :].reshape(slots, 128).astype(f32)
         lane = lax.broadcasted_iota(jnp.int32, (slots, 128), 1).astype(f32)
@@ -162,7 +196,7 @@
         gather_m = jnp.concatenate(
             [jnp.where(ids_t == row + 128.0 * h, 1.0, 0.0) for h in range(slots // 128)], axis=0
         ).astype(bf16)
-        interp_own = interpm[pl.ds(pl.multiple_of(s * share, share), share), :]
+        interp_own = interpm[...]
 
         def raised(cr):
             sorted_pat = dot_nn(
@@ -170,6 +204,15 @@
             ).astype(bf16)
             return dot_nt(sorted_pat, interp_own)
 
+        halos = {
+            (side, r): pltpu.make_async_remote_copy(
+                src_ref=parb.at[r], dst_ref=hbuf.at[side, r],
+                send_sem=h_send.at[side, r], recv_sem=h_recv.at[side, r],
+                device_id=(up_id, down_id)[side], device_id_type=MESH,
+            )
+            for side in range(2)
+            for r in range(4)
+        }
         for r in range(4):
             ar, ai = raised(r), raised(4 + r)
             pr = jnp.zeros((parents, 128), f32)
@@ -179,41 +222,55 @@
                 br, bi = ar[o * parents : (o + 1) * parents], ai[o * parents : (o + 1) * parents]
                 pr = pr + (fr * br - fi * bi)
                 pi = pi + (fr * bi + fi * br)
-            parf[pl.ds(r, parents, stride=8), :] = pr
-            parf[pl.ds(4 + r, parents, stride=8), :] = pi
-        parb[...] = parf[...].astype(bf16)
-
-        to_up = pltpu.make_async_remote_copy(
-            src_ref=parb, dst_ref=hbuf.at[0], send_sem=h_send.at[0], recv_sem=h_recv.at[0],
-            device_id=up_id, device_id_type=MESH,
-        )
-        to_down = pltpu.make_async_remote_copy(
-            src_ref=parb, dst_ref=hbuf.at[1], send_sem=h_send.at[1], recv_sem=h_recv.at[1],
-            device_id=down_id, device_id_type=MESH,
-        )
-        to_up.start()
-        to_down.start()
-        parw[pl.ds(parents, parents)] = parb[...].astype(f32).reshape(parents, 8, 128)
-        to_up.wait()
-        parw[pl.ds(0, parents)] = hbuf[0].astype(f32).reshape(parents, 8, 128)
-        to_down.wait()
-        parw[pl.ds(2 * parents, parents)] = hbuf[1].astype(f32).reshape(parents, 8, 128)
+            parb[r, 0] = pr.astype(bf16)
+            parb[r, 1] = pi.astype(bf16)
+            for side in range(2):
+                halos[side, r].start()
+
+        def keep(block, src):
+            for r in range(4):
+                for c in range(2):
+                    parf[pl.ds(block * pb + 4 * c + r, parents, stride=8), :] = src(r, c).astype(f32)
+            parw[pl.ds(block * parents, parents)] = parf[pl.ds(block * pb, pb), :].reshape(parents, 8, 128)
+
+        keep(1, lambda r, c: parb[r, c])
+        for side in range(2):
+            for r in range(4):
+                halos[side, r].wait()
+            keep(2 * side, lambda r, c: hbuf[side, r, c])
 
         def translate(p, carry):
             s1 = jnp.zeros((8, 128), f32)
             s2 = jnp.zeros((8, 128), f32)
             for k in range(list_k):
-                w = lax.rem(ilist[p, k] - b * parents + parents + total_parents, total_parents)
+                w = lax.rem(ilist[k, p] - b * parents + parents + total_parents, total_parents)
                 v = parw[jnp.minimum(w, 3 * parents - 1)]
-                op = trm[tids[p, k]]
-                s1 = s1 + op[0:1] * v
-                s2 = s2 + op[1:2] * v
+                t = 2 * tids[k, p]
+                s1 = s1 + trb[t] * v
+                s2 = s2 + trb[t + 1] * v
             inc = (s1 + times_i(s2)).astype(bf16).astype(f32)
             incf[pl.ds(pl.multiple_of(p * 8, 8), 8), :] = inc
             return carry
 
         lax.fori_loop(0, parents, translate, 0)
 
+        to_partner = [
+            pltpu.make_async_remote_copy(
+                src_ref=xsend.at[t], dst_ref=xrecv.at[t],
+                send_sem=ax_send.at[t], recv_sem=ax_recv.at[t],
+                device_id=partner, device_id_type=MESH,
+            )
+            for t in range(nz)
+        ]
+        to_owner = {
+            t: pltpu.make_async_remote_copy(
+                src_ref=zsend.at[t], dst_ref=zrecv.at[t],
+                send_sem=az_send.at[t], recv_sem=az_recv.at[t],
+                device_id=along(-t), device_id_type=MESH,
+            )
+            for t in range(1, nz)
+        }
+        rows = slots // 2
         for r in range(4):
             ir = incf[pl.ds(r, parents, stride=8), :]
             ii = incf[pl.ds(4 + r, parents, stride=8), :]
@@ -224,29 +281,27 @@
                 si.append((fr * ii + fi * ir).astype(bf16))
             for cr, part in ((r, sr), (4 + r, si)):
                 u = dot_nn(spread, jnp.concatenate(part, axis=0)).astype(bf16)
-                sbuf[:, pl.ds(cr * boxes, boxes), :] = u.reshape(nsamp, boxes, 128)
-
-        sends = {
-            t: pltpu.make_async_remote_copy(
-                src_ref=sbuf.at[t], dst_ref=rbuf.at[t],
-                send_sem=a_send.at[t], recv_sem=a_recv.at[t],
-                device_id=peer(-t), device_id_type=MESH,
-            )
-            for t in range(1, nsamp)
-        }
+                low = dot_nn(u, interp_own)
+                ownf[:, pl.ds(cr * boxes, boxes), :] = low[:rows].reshape(nz, boxes, 128)
+                xsend[:, pl.ds(cr * boxes, boxes), :] = low[rows:].astype(bf16).reshape(nz, boxes, 128)
         for t in order:
-            sends[t].start()
-
-        lax.fori_loop(boxes // 2, boxes, near_box, 0)
-
-        def lowered(t, block):
-            j = lax.rem(s + t, nsamp)
-            return dot_nn(block, interpm[pl.ds(pl.multiple_of(j * share, share), share), :])
-
-        field = lowered(0, sbuf[0])
-        for t in sorted(range(1, nsamp), key=lambda t: min(t, nsamp - t)):
-            sends[t].wait()
-            field = field + lowered(t, rbuf[t])
+            to_partner[t].start()
+        to_partner[0].start()
+        done = boxes // 2
+        for i, t in enumerate(order):
+            to_partner[t].wait_recv()
+            zsend[t] = (ownf[t] + xrecv[t].astype(f32)).astype(bf16)
+            to_owner[t].start()
+            upto = boxes // 2 + boxes * (i + 1) // (2 * len(order))
+            lax.fori_loop(done, upto, near_box, 0)
+            done = upto
+        to_partner[0].wait_recv()
+        field = ownf[0] + xrecv[0].astype(f32)
+        for t in range(nz):
+            to_partner[t].wait_send()
+        for t in order[::-1]:
+            to_owner[t].wait()
+            field = field + zrecv[t].astype(f32)
         fieldf[...] = field
         place_cp.wait()
         for n in range(boxes):
@@ -267,6 +322,7 @@
     parents = inter_list.shape[0]
     share = interp.shape[0] // nsamp
     blk = boxes * 8
+    nz = nsamp // 2
     x2 = xvec.reshape(blk, 128)
     smem = pl.BlockSpec(memory_space=pltpu.SMEM)
     hbm = pl.BlockSpec(memory_space=pltpu.HBM)
@@ -282,33 +338,38 @@
             pltpu.VMEM(near_blocks.shape, bf16),
             pltpu.VMEM(lift.shape, bf16),
             pltpu.VMEM(place.shape, bf16),
-            pltpu.VMEM(interp.shape, bf16),
+            pltpu.VMEM((share, interp.shape[1]), bf16),
             pltpu.VMEM((8, 2, share), f32),
             pltpu.VMEM(translators.shape, f32),
+            pltpu.VMEM((2 * translators.shape[0], 8, 128), f32),
             pltpu.VMEM((blk, 128), f32),
             pltpu.VMEM((boxes, 128), f32),
             pltpu.VMEM((nsamp, blk + boxes, 128), bf16),
+            pltpu.VMEM((3 * parents * 8, 128), f32),
+            pltpu.VMEM((3 * parents, 8, 128), f32),
+            pltpu.VMEM((4, 2, parents, 128), bf16),
+            pltpu.VMEM((2, 4, 2, parents, 128), bf16),
             pltpu.VMEM((parents * 8, 128), f32),
-            pltpu.VMEM((3 * parents, 8, 128), f32),
-            pltpu.VMEM((parents * 8, 128), bf16),
-            pltpu.VMEM((2, parents * 8, 128), bf16),
-            pltpu.VMEM((parents * 8, 128), f32),
-            pltpu.VMEM((nsamp, blk, 128), bf16),
-            pltpu.VMEM((nsamp, blk, 128), bf16),
+            pltpu.VMEM((nz, blk, 128), f32),
+            pltpu.VMEM((nz, blk, 128), bf16),
+            pltpu.VMEM((nz, blk, 128), bf16),
+            pltpu.VMEM((nz, blk, 128), bf16),
+            pltpu.VMEM((nz, blk, 128), bf16),
             pltpu.VMEM((blk, 128), f32),
             pltpu.VMEM((blk, 128), f32),
             dma((boxes,)),
             dma((6,)),
             dma((2,)), dma((2,)),
             dma((nsamp,)), dma((nsamp,)),
-            dma((2,)), dma((2,)),
-            dma((nsamp,)), dma((nsamp,)),
+            dma((2, 4)), dma((2, 4)),
+            dma((nz,)), dma((nz,)),
+            dma((nz,)), dma((nz,)),
         ],
         compiler_params=pltpu.CompilerParams(
             collective_id=0, has_side_effects=True, vmem_limit_bytes=60 * 1024 * 1024
         ),
     )(
-        neighbours, octant, leaf_parent_index, inter_list, trans_id,
+        neighbours.T, octant, leaf_parent_index, inter_list.T, trans_id.T,
         x2, near_blocks, lift, place, interp, phases, translators,
     )
     return out.reshape(xvec.shape)

time: 58.8 us -> 48.6 us (0.83)
  the two profiles are of different devices: /device:TPU:1 before, /device:TPU:2 now
where the time goes in v2:
time: 48.6 us; the launch traced here: 48.4 us
  Pallas kernels  46.9 us (97%)
  local copies, waits for them, and re-layouts  1.47 us (3%)
    pallas_call x1, Pallas kernels, on_device(): pl.pallas_call(make_kernel(nbox, nsamp, boxes, parents, neighbours.shape[...  46.9 us
    unnamed x1, local copies, waits for them, and re-layouts  1.47 us

profile of v2, /device:TPU:2, one launch (start us, length us, event | category | flops | bytes accessed | tf_op | source)
XLA Modules:
  0.0 48.4 jit_solution(13736665224489566782)
XLA Ops:
  0.0 46.9 %shard_map.118 = f32[128,128]{1,0:T(8,128)} custom-call(s32[8,16]{1,0:T(8,128)} %bitcast.9, s32[16]{0:T(128)} %octs.1, s32[16]{0:T(128)} %pars.1, s32[16,32]{1,0:T(8,128)} %bitcast.7, s32[16,32]{1,0:T(8,128)} %bitcast.8, bf16[128,128]{1,0:T(8,128)(2,1)} %bitcast.6, bf16[16,8,2,128,128]{4,3,2,1,0:T(8,128)(2,1)} %near_hbm.1, ...), custom_call_target="tpu_custom_call" | custom-call | tf_op jit(solution)/shard_map/pallas_call | solution.py:330
  46.9 1.5 %copy.14 = f32[16,2,4,128]{3,2,1,0:T(4,128)} copy(f32[16,2,4,128]{3,2,1,0:T(4,128)} %bitcast.5) | data formatting | bytes 131072

commit v3 on v2

--- a/solution.py
+++ b/solution.py
@@ -33,16 +33,18 @@
     pb = parents * 8
     slots = boxes * nsamp
     nz = nsamp // 2
+    half_rows = blk // 2
     share = sample_share
 
     def kernel(
-        nbr, octs, pars, ilist, tids,
+        nbr_hbm, octs_hbm, pars_hbm, ilist_hbm, tids_hbm,
         x_hbm, near_hbm, lift_hbm, place_hbm, interp_hbm, phases_hbm, trans_hbm,
         out,
+        nbr, octs, pars, ilist, tids, wtab,
         xh, xf, nearm, liftm, placem, interpm, phm, trm, trb,
         patf, slotf, gbuf, parf, parw, parb, hbuf, incf,
         ownf, xsend, xrecv, zsend, zrecv, nearf, fieldf,
-        near_sem, in_sem,
+        near_sem, in_sem, idx_sem,
         halo_send, halo_recv, g_send, g_recv, h_send, h_recv,
         ax_send, ax_recv, az_send, az_recv,
     ):
@@ -64,8 +66,16 @@
         near_cps = [
             pltpu.make_async_copy(near_hbm.at[n], nearm.at[n], near_sem.at[n]) for n in range(boxes)
         ]
+        idx_cps = [
+            pltpu.make_async_copy(src, dst, idx_sem.at[i])
+            for i, (src, dst) in enumerate(
+                ((octs_hbm, octs), (pars_hbm, pars), (nbr_hbm, nbr), (ilist_hbm, ilist), (tids_hbm, tids))
+            )
+        ]
         x_cp.start()
         lift_cp.start()
+        for cp in idx_cps:
+            cp.start()
 
         barrier = pltpu.get_barrier_semaphore()
         right = lax.rem(me + 1, ndev)
@@ -95,6 +105,8 @@
         for cp in near_cps[boxes // 2 :]:
             cp.start()
 
+        idx_cps[0].wait()
+        idx_cps[1].wait()
         for n in range(boxes):
             slot = octs[n] * parents + (pars[n] - b * parents)
             slotf[pl.ds(n, 1), :] = jnp.full((1, 128), slot, jnp.int32).astype(f32)
@@ -145,6 +157,16 @@
             gathers[t].start()
         gathers[nz].start()
 
+        for cp in idx_cps[2:]:
+            cp.wait()
+
+        def window(p, carry):
+            for k in range(list_k):
+                w = lax.rem(ilist[k, p] - b * parents + parents + total_parents, total_parents)
+                wtab[k, p] = jnp.minimum(w, 3 * parents - 1)
+            return carry
+
+        lax.fori_loop(0, parents, window, 0)
         to_right.wait()
         to_left.wait()
         xf[pl.ds(0, half)] = xh[pl.ds(0, half * 8), :].astype(f32).reshape(half, 8, 128)
@@ -243,8 +265,7 @@
             s1 = jnp.zeros((8, 128), f32)
             s2 = jnp.zeros((8, 128), f32)
             for k in range(list_k):
-                w = lax.rem(ilist[k, p] - b * parents + parents + total_parents, total_parents)
-                v = parw[jnp.minimum(w, 3 * parents - 1)]
+                v = parw[wtab[k, p]]
                 t = 2 * tids[k, p]
                 s1 = s1 + trb[t] * v
                 s2 = s2 + trb[t + 1] * v
@@ -252,16 +273,18 @@
             incf[pl.ds(pl.multiple_of(p * 8, 8), 8), :] = inc
             return carry
 
-        lax.fori_loop(0, parents, translate, 0)
-
-        to_partner = [
-            pltpu.make_async_remote_copy(
-                src_ref=xsend.at[t], dst_ref=xrecv.at[t],
-                send_sem=ax_send.at[t], recv_sem=ax_recv.at[t],
+        lax.fori_loop(0, parents, translate, 0, unroll=4)
+
+        to_partner = {
+            (t, h): pltpu.make_async_remote_copy(
+                src_ref=xsend.at[t, pl.ds(h * half_rows, half_rows)],
+                dst_ref=xrecv.at[t, pl.ds(h * half_rows, half_rows)],
+                send_sem=ax_send.at[t, h], recv_sem=ax_recv.at[t, h],
                 device_id=partner, device_id_type=MESH,
             )
             for t in range(nz)
-        ]
+            for h in range(2)
+        }
         to_owner = {
             t: pltpu.make_async_remote_copy(
                 src_ref=zsend.at[t], dst_ref=zrecv.at[t],
@@ -271,6 +294,7 @@
             for t in range(1, nz)
         }
         rows = slots // 2
+        turn = order + [0]
         for r in range(4):
             ir = incf[pl.ds(r, parents, stride=8), :]
             ii = incf[pl.ds(4 + r, parents, stride=8), :]
@@ -279,30 +303,37 @@
                 fr, fi = phm[o, pl.ds(0, 1), :], phm[o, pl.ds(1, 1), :]
                 sr.append((fr * ir - fi * ii).astype(bf16))
                 si.append((fr * ii + fi * ir).astype(bf16))
-            for cr, part in ((r, sr), (4 + r, si)):
+            for cr, part in ((2 * r, sr), (2 * r + 1, si)):
                 u = dot_nn(spread, jnp.concatenate(part, axis=0)).astype(bf16)
                 low = dot_nn(u, interp_own)
                 ownf[:, pl.ds(cr * boxes, boxes), :] = low[:rows].reshape(nz, boxes, 128)
                 xsend[:, pl.ds(cr * boxes, boxes), :] = low[rows:].astype(bf16).reshape(nz, boxes, 128)
-        for t in order:
-            to_partner[t].start()
-        to_partner[0].start()
+            if r % 2 == 1:
+                for t in turn:
+                    to_partner[t, r // 2].start()
         done = boxes // 2
         for i, t in enumerate(order):
-            to_partner[t].wait_recv()
+            for h in range(2):
+                to_partner[t, h].wait_recv()
             zsend[t] = (ownf[t] + xrecv[t].astype(f32)).astype(bf16)
             to_owner[t].start()
             upto = boxes // 2 + boxes * (i + 1) // (2 * len(order))
             lax.fori_loop(done, upto, near_box, 0)
             done = upto
-        to_partner[0].wait_recv()
+        for h in range(2):
+            to_partner[0, h].wait_recv()
         field = ownf[0] + xrecv[0].astype(f32)
         for t in range(nz):
-            to_partner[t].wait_send()
+            for h in range(2):
+                to_partner[t, h].wait_send()
         for t in order[::-1]:
             to_owner[t].wait()
             field = field + zrecv[t].astype(f32)
-        fieldf[...] = field
+        for r in range(4):
+            for c in range(2):
+                fieldf[pl.ds((4 * c + r) * boxes, boxes), :] = (
+                    field[(2 * r + c) * boxes : (2 * r + c + 1) * boxes]
+                )
         place_cp.wait()
         for n in range(boxes):
             fn = fieldf[pl.ds(n, 8, stride=boxes), :].astype(bf16)
@@ -324,15 +355,20 @@
     blk = boxes * 8
     nz = nsamp // 2
     x2 = xvec.reshape(blk, 128)
-    smem = pl.BlockSpec(memory_space=pltpu.SMEM)
     hbm = pl.BlockSpec(memory_space=pltpu.HBM)
     dma = pltpu.SemaphoreType.DMA
     out = pl.pallas_call(
         make_kernel(nbox, nsamp, boxes, parents, neighbours.shape[1], inter_list.shape[1], share),
         out_shape=jax.ShapeDtypeStruct((blk, 128), f32),
-        in_specs=[smem] * 5 + [hbm] * 7,
+        in_specs=[hbm] * 12,
         out_specs=pl.BlockSpec(memory_space=pltpu.VMEM),
         scratch_shapes=[
+            pltpu.SMEM(neighbours.shape[::-1], jnp.int32),
+            pltpu.SMEM(octant.shape, jnp.int32),
+            pltpu.SMEM(octant.shape, jnp.int32),
+            pltpu.SMEM(inter_list.shape[::-1], jnp.int32),
+            pltpu.SMEM(inter_list.shape[::-1], jnp.int32),
+            pltpu.SMEM(inter_list.shape[::-1], jnp.int32),
             pltpu.VMEM((2 * blk, 128), bf16),
             pltpu.VMEM((2 * boxes, 8, 128), f32),
             pltpu.VMEM(near_blocks.shape, bf16),
@@ -358,19 +394,24 @@
             pltpu.VMEM((blk, 128), f32),
             pltpu.VMEM((blk, 128), f32),
             dma((boxes,)),
-            dma((6,)),
+            dma((6,)), dma((5,)),
             dma((2,)), dma((2,)),
             dma((nsamp,)), dma((nsamp,)),
             dma((2, 4)), dma((2, 4)),
-            dma((nz,)), dma((nz,)),
+            dma((nz, 2)), dma((nz, 2)),
             dma((nz,)), dma((nz,)),
         ],
         compiler_params=pltpu.CompilerParams(
-            collective_id=0, has_side_effects=True, vmem_limit_bytes=60 * 1024 * 1024
+            collective_id=0, has_side_effects=True, vmem_limit_bytes=48 * 1024 * 1024
         ),
     )(
-        neighbours.T, octant, leaf_parent_index, inter_list.T, trans_id.T,
-        x2, near_blocks, lift, place, interp, phases, translators,
+        *[
+            pltpu.with_memory_space_constraint(a, pltpu.HBM)
+            for a in (
+                neighbours.T, octant, leaf_parent_index, inter_list.T, trans_id.T,
+                x2, near_blocks, lift, place, interp, phases, translators,
+            )
+        ]
     )
     return out.reshape(xvec.shape)
 

time: 48.6 us -> 45.5 us (0.936)
  Pallas kernels: 46.9 us -> 44.5 us
  local copies, waits for them, and re-layouts: 1.47 us -> 0.63 us
    pallas_call x1, Pallas kernels: 46.9 us -> 44.5 us  [on_device(): pl.pallas_call(make_kernel(nbox, nsamp, boxes, parents, neighbours.shape[...]
    unnamed x1, local copies, waits for them, and re-layouts: 1.47 us -> 0.63 us
where the time goes in v3:
time: 45.5 us; the launch traced here: 45.2 us
  Pallas kernels  44.5 us (98%)
  local copies, waits for them, and re-layouts  0.63 us (1%)
    pallas_call x1, Pallas kernels, on_device(): pl.pallas_call(make_kernel(nbox, nsamp, boxes, parents, neighbours.shape[...  44.5 us

profile of v3, /device:TPU:2, one launch (start us, length us, event | category | flops | bytes accessed | tf_op | source)
XLA Modules:
  0.0 45.2 jit_solution(217266298122611716)
XLA Ops:
  0.0 44.5 %shard_map.118 = f32[128,128]{1,0:T(8,128)S(1)} custom-call(s32[8,16]{1,0:T(8,128)} %bitcast.9, s32[16]{0:T(128)} %octs_hbm.1, s32[16]{0:T(128)} %pars_hbm.1, s32[16,32]{1,0:T(8,128)} %bitcast.7, s32[16,32]{1,0:T(8,128)} %bitcast.8, bf16[128,128]{1,0:T(8,128)(2,1)} %bitcast.6, bf16[16,8,2,128,128]{4,3,2,1,0:T(8,128)(2,1)} %near_hbm.1, ...), custom_call_target="tpu_custom_call" | custom-call | tf_op jit(solution)/shard_map/pallas_call | solution.py:360
  44.5 0.6 %copy.14 = f32[16,2,4,128]{3,2,1,0:T(4,128)} copy(f32[16,2,4,128]{3,2,1,0:T(4,128)S(1)} %bitcast.5) | data formatting | bytes 131072

commit v4 on v3

--- a/solution.py
+++ b/solution.py
@@ -34,6 +34,8 @@
     slots = boxes * nsamp
     nz = nsamp // 2
     half_rows = blk // 2
+    relay_out = (7, 6, 1)
+    relay_back = (1, 2, 7)
     share = sample_share
 
     def kernel(
@@ -41,12 +43,12 @@
         x_hbm, near_hbm, lift_hbm, place_hbm, interp_hbm, phases_hbm, trans_hbm,
         out,
         nbr, octs, pars, ilist, tids, wtab,
-        xh, xf, nearm, liftm, placem, interpm, phm, trm, trb,
+        xh, xf, nearm, liftm, placem, interpm, twin, phm, trm, trb,
         patf, slotf, gbuf, parf, parw, parb, hbuf, incf,
-        ownf, xsend, xrecv, zsend, zrecv, nearf, fieldf,
+        ownf, crossf, xsend, xrecv, brecv, zsend, zrecv, nearf, fieldf,
         near_sem, in_sem, idx_sem,
         halo_send, halo_recv, g_send, g_recv, h_send, h_recv,
-        ax_send, ax_recv, az_send, az_recv,
+        ax_send, ax_recv, b_send, b_recv, az_send, az_recv,
     ):
         b = lax.axis_index("box")
         s = lax.axis_index("samp")
@@ -151,11 +153,18 @@
                 device_id=partner, device_id_type=MESH,
             )
 
+        def pass_on(t):
+            return pltpu.make_async_remote_copy(
+                src_ref=gbuf.at[nz], dst_ref=gbuf.at[nz + t],
+                send_sem=g_send.at[nz + t], recv_sem=g_recv.at[nz + t],
+                device_id=along(t), device_id_type=MESH,
+            )
+
         gathers = {t: spread_out(t) for t in order}
-        gathers.update({nz + t: hand_over(t) for t in range(nz)})
+        gathers.update({nz + t: pass_on(t) if t in relay_out else hand_over(t) for t in range(nz)})
+        gathers[nz].start()
         for t in order:
             gathers[t].start()
-        gathers[nz].start()
 
         for cp in idx_cps[2:]:
             cp.wait()
@@ -184,15 +193,23 @@
             nearf[pl.ds(pl.multiple_of(n * 8, 8), 8), :] = acc[:, :128] + times_i(acc[:, 128:])
             return carry
 
-        done = 0
+        lax.fori_loop(0, 3, near_box, 0)
+        gathers[nz].wait_recv()
+        for t in relay_out:
+            gathers[nz + t].start()
+        done = 3
         for i, t in enumerate(order):
-            upto = boxes * (i + 1) // (2 * len(order))
+            upto = 3 + (boxes // 2 - 3) * (i + 1) // len(order)
             lax.fori_loop(done, upto, near_box, 0)
             done = upto
             gathers[t].wait_recv()
-            gathers[nz + t].start()
+            if t not in relay_out:
+                gathers[nz + t].start()
 
         interp_cp.wait()
+        twin[...] = jnp.zeros(twin.shape, bf16)
+        twin[pl.ds(0, share), pl.ds(0, 128)] = interpm[...]
+        twin[pl.ds(share, share), pl.ds(128, 128)] = interpm[...]
         ph_cp.wait()
         tr_cp.wait()
 
@@ -205,7 +222,8 @@
         lax.fori_loop(0, trm.shape[0], widen, 0, unroll=8)
         for t in order:
             gathers[t].wait_send()
-        for t in range(nz):
+        gathers[nz].wait_send()
+        for t in order:
             gathers[nz + t].wait()
 
         ids = gbuf[:, pl.ds(blk, boxes), :].reshape(slots, 128).astype(f32)
@@ -218,13 +236,16 @@
         gather_m = jnp.concatenate(
             [jnp.where(ids_t == row + 128.0 * h, 1.0, 0.0) for h in range(slots // 128)], axis=0
         ).astype(bf16)
-        interp_own = interpm[...]
-
-        def raised(cr):
-            sorted_pat = dot_nn(
-                gather_m, gbuf[:, pl.ds(cr * boxes, boxes), :].reshape(slots, 128)
-            ).astype(bf16)
-            return dot_nt(sorted_pat, interp_own)
+
+        def raised(r):
+            pair = jnp.concatenate(
+                [
+                    gbuf[:, pl.ds(cr * boxes, boxes), :].reshape(slots, 128)
+                    for cr in (r, 4 + r)
+                ],
+                axis=1,
+            )
+            return dot_nt(dot_nn(gather_m, pair).astype(bf16), twin[...])
 
         halos = {
             (side, r): pltpu.make_async_remote_copy(
@@ -236,7 +257,8 @@
             for r in range(4)
         }
         for r in range(4):
-            ar, ai = raised(r), raised(4 + r)
+            both = raised(r)
+            ar, ai = both[:, :128], both[:, 128:]
             pr = jnp.zeros((parents, 128), f32)
             pi = jnp.zeros((parents, 128), f32)
             for o in range(8):
@@ -275,6 +297,7 @@
 
         lax.fori_loop(0, parents, translate, 0, unroll=4)
 
+        turn = [t for t in order if t not in relay_back] + [0]
         to_partner = {
             (t, h): pltpu.make_async_remote_copy(
                 src_ref=xsend.at[t, pl.ds(h * half_rows, half_rows)],
@@ -282,8 +305,16 @@
                 send_sem=ax_send.at[t, h], recv_sem=ax_recv.at[t, h],
                 device_id=partner, device_id_type=MESH,
             )
-            for t in range(nz)
+            for t in turn
             for h in range(2)
+        }
+        to_relay = {
+            t: pltpu.make_async_remote_copy(
+                src_ref=xsend.at[t], dst_ref=brecv.at[t],
+                send_sem=b_send.at[t], recv_sem=b_recv.at[t],
+                device_id=along(-t), device_id_type=MESH,
+            )
+            for t in relay_back
         }
         to_owner = {
             t: pltpu.make_async_remote_copy(
@@ -294,7 +325,6 @@
             for t in range(1, nz)
         }
         rows = slots // 2
-        turn = order + [0]
         for r in range(4):
             ir = incf[pl.ds(r, parents, stride=8), :]
             ii = incf[pl.ds(4 + r, parents, stride=8), :]
@@ -303,29 +333,46 @@
                 fr, fi = phm[o, pl.ds(0, 1), :], phm[o, pl.ds(1, 1), :]
                 sr.append((fr * ir - fi * ii).astype(bf16))
                 si.append((fr * ii + fi * ir).astype(bf16))
-            for cr, part in ((2 * r, sr), (2 * r + 1, si)):
-                u = dot_nn(spread, jnp.concatenate(part, axis=0)).astype(bf16)
-                low = dot_nn(u, interp_own)
+            pair = jnp.concatenate([jnp.concatenate(sr, axis=0), jnp.concatenate(si, axis=0)], axis=1)
+            both = dot_nn(dot_nn(spread, pair).astype(bf16), twin[...])
+            for cr, low in ((2 * r, both[:, :128]), (2 * r + 1, both[:, 128:])):
                 ownf[:, pl.ds(cr * boxes, boxes), :] = low[:rows].reshape(nz, boxes, 128)
                 xsend[:, pl.ds(cr * boxes, boxes), :] = low[rows:].astype(bf16).reshape(nz, boxes, 128)
+                crossf[pl.ds(cr * boxes, boxes), :] = low[rows : rows + boxes]
             if r % 2 == 1:
-                for t in turn:
+                for t in turn[:-1]:
                     to_partner[t, r // 2].start()
-        done = boxes // 2
-        for i, t in enumerate(order):
+        for t in relay_back:
+            to_relay[t].start()
+        for t in relay_back:
+            zsend[t] = ownf[t].astype(bf16)
+            to_owner[t].start()
+
+        def add_partner(t):
             for h in range(2):
                 to_partner[t, h].wait_recv()
             zsend[t] = (ownf[t] + xrecv[t].astype(f32)).astype(bf16)
             to_owner[t].start()
-            upto = boxes // 2 + boxes * (i + 1) // (2 * len(order))
-            lax.fori_loop(done, upto, near_box, 0)
-            done = upto
+
+        add_partner(turn[0])
+        cross = crossf[...]
+        for t in relay_back:
+            to_relay[t].wait_recv()
+            cross = cross + brecv[t].astype(f32)
+        xsend[0] = cross.astype(bf16)
+        for h in range(2):
+            to_partner[0, h].start()
+        for t in turn[1:-1]:
+            add_partner(t)
+        lax.fori_loop(boxes // 2, boxes, near_box, 0)
         for h in range(2):
             to_partner[0, h].wait_recv()
         field = ownf[0] + xrecv[0].astype(f32)
-        for t in range(nz):
+        for t in turn:
             for h in range(2):
                 to_partner[t, h].wait_send()
+        for t in relay_back:
+            to_relay[t].wait_send()
         for t in order[::-1]:
             to_owner[t].wait()
             field = field + zrecv[t].astype(f32)
@@ -375,6 +422,7 @@
             pltpu.VMEM(lift.shape, bf16),
             pltpu.VMEM(place.shape, bf16),
             pltpu.VMEM((share, interp.shape[1]), bf16),
+            pltpu.VMEM((2 * share, 2 * interp.shape[1]), bf16),
             pltpu.VMEM((8, 2, share), f32),
             pltpu.VMEM(translators.shape, f32),
             pltpu.VMEM((2 * translators.shape[0], 8, 128), f32),
@@ -387,6 +435,8 @@
             pltpu.VMEM((2, 4, 2, parents, 128), bf16),
             pltpu.VMEM((parents * 8, 128), f32),
             pltpu.VMEM((nz, blk, 128), f32),
+            pltpu.VMEM((blk, 128), f32),
+            pltpu.VMEM((nz, blk, 128), bf16),
             pltpu.VMEM((nz, blk, 128), bf16),
             pltpu.VMEM((nz, blk, 128), bf16),
             pltpu.VMEM((nz, blk, 128), bf16),
@@ -399,6 +449,7 @@
             dma((nsamp,)), dma((nsamp,)),
             dma((2, 4)), dma((2, 4)),
             dma((nz, 2)), dma((nz, 2)),
+            dma((nz,)), dma((nz,)),
             dma((nz,)), dma((nz,)),
         ],
         compiler_params=pltpu.CompilerParams(

time: 45.5 us -> 40.6 us (0.89)
  Pallas kernels: 44.5 us -> 39.9 us
    pallas_call x1, Pallas kernels: 44.5 us -> 39.9 us  [on_device(): pl.pallas_call(make_kernel(nbox, nsamp, boxes, parents, neighbours.shape[...]
where the time goes in v4:
time: 40.6 us; the launch traced here: 40.5 us
  Pallas kernels  39.9 us (98%)
  local copies, waits for them, and re-layouts  0.63 us (2%)
    pallas_call x1, Pallas kernels, on_device(): pl.pallas_call(make_kernel(nbox, nsamp, boxes, parents, neighbours.shape[...  39.9 us

profile of v4, /device:TPU:2, one launch (start us, length us, event | category | flops | bytes accessed | tf_op | source)
XLA Modules:
  0.0 40.5 jit_solution(966945669521746756)
XLA Ops:
  0.0 39.9 %shard_map.118 = f32[128,128]{1,0:T(8,128)S(1)} custom-call(s32[8,16]{1,0:T(8,128)} %bitcast.9, s32[16]{0:T(128)} %octs_hbm.1, s32[16]{0:T(128)} %pars_hbm.1, s32[16,32]{1,0:T(8,128)} %bitcast.7, s32[16,32]{1,0:T(8,128)} %bitcast.8, bf16[128,128]{1,0:T(8,128)(2,1)} %bitcast.6, bf16[16,8,2,128,128]{4,3,2,1,0:T(8,128)(2,1)} %near_hbm.1, ...), custom_call_target="tpu_custom_call" | custom-call | tf_op jit(solution)/shard_map/pallas_call | solution.py:407
  39.9 0.6 %copy.14 = f32[16,2,4,128]{3,2,1,0:T(4,128)} copy(f32[16,2,4,128]{3,2,1,0:T(4,128)S(1)} %bitcast.5) | data formatting | bytes 131072

commit v5 on v4

--- a/solution.py
+++ b/solution.py
@@ -34,8 +34,8 @@
     slots = boxes * nsamp
     nz = nsamp // 2
     half_rows = blk // 2
-    relay_out = (7, 6, 1)
-    relay_back = (1, 2, 7)
+    relay_out = (7, 6, 1, 2)
+    relay_back = (1, 2, 7, 6)
     share = sample_share
 
     def kernel(
@@ -248,13 +248,12 @@
             return dot_nt(dot_nn(gather_m, pair).astype(bf16), twin[...])
 
         halos = {
-            (side, r): pltpu.make_async_remote_copy(
-                src_ref=parb.at[r], dst_ref=hbuf.at[side, r],
-                send_sem=h_send.at[side, r], recv_sem=h_recv.at[side, r],
+            side: pltpu.make_async_remote_copy(
+                src_ref=parb, dst_ref=hbuf.at[side],
+                send_sem=h_send.at[side, 0], recv_sem=h_recv.at[side, 0],
                 device_id=(up_id, down_id)[side], device_id_type=MESH,
             )
             for side in range(2)
-            for r in range(4)
         }
         for r in range(4):
             both = raised(r)
@@ -268,8 +267,9 @@
                 pi = pi + (fr * bi + fi * br)
             parb[r, 0] = pr.astype(bf16)
             parb[r, 1] = pi.astype(bf16)
-            for side in range(2):
-                halos[side, r].start()
+            if r == 3:
+                for side in range(2):
+                    halos[side].start()
 
         def keep(block, src):
             for r in range(4):
@@ -279,8 +279,7 @@
 
         keep(1, lambda r, c: parb[r, c])
         for side in range(2):
-            for r in range(4):
-                halos[side, r].wait()
+            halos[side].wait()
             keep(2 * side, lambda r, c: hbuf[side, r, c])
 
         def translate(p, carry):
@@ -299,14 +298,12 @@
 
         turn = [t for t in order if t not in relay_back] + [0]
         to_partner = {
-            (t, h): pltpu.make_async_remote_copy(
-                src_ref=xsend.at[t, pl.ds(h * half_rows, half_rows)],
-                dst_ref=xrecv.at[t, pl.ds(h * half_rows, half_rows)],
-                send_sem=ax_send.at[t, h], recv_sem=ax_recv.at[t, h],
+            t: pltpu.make_async_remote_copy(
+                src_ref=xsend.at[t], dst_ref=xrecv.at[t],
+                send_sem=ax_send.at[t, 0], recv_sem=ax_recv.at[t, 0],
                 device_id=partner, device_id_type=MESH,
             )
             for t in turn
-            for h in range(2)
         }
         to_relay = {
             t: pltpu.make_async_remote_copy(
@@ -339,9 +336,9 @@
                 ownf[:, pl.ds(cr * boxes, boxes), :] = low[:rows].reshape(nz, boxes, 128)
                 xsend[:, pl.ds(cr * boxes, boxes), :] = low[rows:].astype(bf16).reshape(nz, boxes, 128)
                 crossf[pl.ds(cr * boxes, boxes), :] = low[rows : rows + boxes]
-            if r % 2 == 1:
+            if r == 3:
                 for t in turn[:-1]:
-                    to_partner[t, r // 2].start()
+                    to_partner[t].start()
         for t in relay_back:
             to_relay[t].start()
         for t in relay_back:
@@ -349,8 +346,7 @@
             to_owner[t].start()
 
         def add_partner(t):
-            for h in range(2):
-                to_partner[t, h].wait_recv()
+            to_partner[t].wait_recv()
             zsend[t] = (ownf[t] + xrecv[t].astype(f32)).astype(bf16)
             to_owner[t].start()
 
@@ -360,17 +356,14 @@
             to_relay[t].wait_recv()
             cross = cross + brecv[t].astype(f32)
         xsend[0] = cross.astype(bf16)
-        for h in range(2):
-            to_partner[0, h].start()
+        to_partner[0].start()
         for t in turn[1:-1]:
             add_partner(t)
         lax.fori_loop(boxes // 2, boxes, near_box, 0)
-        for h in range(2):
-            to_partner[0, h].wait_recv()
+        to_partner[0].wait_recv()
         field = ownf[0] + xrecv[0].astype(f32)
         for t in turn:
-            for h in range(2):
-                to_partner[t, h].wait_send()
+            to_partner[t].wait_send()
         for t in relay_back:
             to_relay[t].wait_send()
         for t in order[::-1]:

time: 40.6 us -> 39.7 us (0.978)
  Pallas kernels: 39.9 us -> 39 us
    pallas_call x1, Pallas kernels: 39.9 us -> 39 us  [on_device(): pl.pallas_call(make_kernel(nbox, nsamp, boxes, parents, neighbours.shape[...]
where the time goes in v5:
time: 39.7 us; the launch traced here: 39.6 us
  Pallas kernels  39 us (98%)
  local copies, waits for them, and re-layouts  0.63 us (2%)
    pallas_call x1, Pallas kernels, on_device(): pl.pallas_call(make_kernel(nbox, nsamp, boxes, parents, neighbours.shape[...  39 us

profile of v5, /device:TPU:2, one launch (start us, length us, event | category | flops | bytes accessed | tf_op | source)
XLA Modules:
  0.0 39.6 jit_solution(66113703549290587)
XLA Ops:
  0.0 39.0 %shard_map.118 = f32[128,128]{1,0:T(8,128)S(1)} custom-call(s32[8,16]{1,0:T(8,128)} %bitcast.9, s32[16]{0:T(128)} %octs_hbm.1, s32[16]{0:T(128)} %pars_hbm.1, s32[16,32]{1,0:T(8,128)} %bitcast.7, s32[16,32]{1,0:T(8,128)} %bitcast.8, bf16[128,128]{1,0:T(8,128)(2,1)} %bitcast.6, bf16[16,8,2,128,128]{4,3,2,1,0:T(8,128)(2,1)} %near_hbm.1, ...), custom_call_target="tpu_custom_call" | custom-call | tf_op jit(solution)/shard_map/pallas_call | solution.py:400
  39.0 0.6 %copy.14 = f32[16,2,4,128]{3,2,1,0:T(4,128)} copy(f32[16,2,4,128]{3,2,1,0:T(4,128)S(1)} %bitcast.5) | data formatting | bytes 131072

commit v6 on v5

--- a/solution.py
+++ b/solution.py
@@ -294,7 +294,7 @@
             incf[pl.ds(pl.multiple_of(p * 8, 8), 8), :] = inc
             return carry
 
-        lax.fori_loop(0, parents, translate, 0, unroll=4)
+        lax.fori_loop(0, parents, translate, 0, unroll=8)
 
         turn = [t for t in order if t not in relay_back] + [0]
         to_partner = {
@@ -336,11 +336,10 @@
                 ownf[:, pl.ds(cr * boxes, boxes), :] = low[:rows].reshape(nz, boxes, 128)
                 xsend[:, pl.ds(cr * boxes, boxes), :] = low[rows:].astype(bf16).reshape(nz, boxes, 128)
                 crossf[pl.ds(cr * boxes, boxes), :] = low[rows : rows + boxes]
-            if r == 3:
-                for t in turn[:-1]:
-                    to_partner[t].start()
         for t in relay_back:
             to_relay[t].start()
+        for t in turn[:-1]:
+            to_partner[t].start()
         for t in relay_back:
             zsend[t] = ownf[t].astype(bf16)
             to_owner[t].start()
@@ -350,14 +349,13 @@
             zsend[t] = (ownf[t] + xrecv[t].astype(f32)).astype(bf16)
             to_owner[t].start()
 
-        add_partner(turn[0])
         cross = crossf[...]
         for t in relay_back:
             to_relay[t].wait_recv()
             cross = cross + brecv[t].astype(f32)
         xsend[0] = cross.astype(bf16)
         to_partner[0].start()
-        for t in turn[1:-1]:
+        for t in turn[:-1]:
             add_partner(t)
         lax.fori_loop(boxes // 2, boxes, near_box, 0)
         to_partner[0].wait_recv()

time: 39.7 us -> 39.7 us (level)
  no operation moved by 1% of the time
where the time goes in v6:
time: 39.7 us
  Pallas kernels  39 us (98%)
  local copies, waits for them, and re-layouts  0.63 us (2%)
    pallas_call x1, Pallas kernels, on_device(): pl.pallas_call(make_kernel(nbox, nsamp, boxes, parents, neighbours.shape[...  39 us

profile of v6, /device:TPU:2, one launch (start us, length us, event | category | flops | bytes accessed | tf_op | source)
XLA Modules:
  0.0 39.7 jit_solution(10768844937121626494)
XLA Ops:
  0.0 39.0 %shard_map.118 = f32[128,128]{1,0:T(8,128)S(1)} custom-call(s32[8,16]{1,0:T(8,128)} %bitcast.9, s32[16]{0:T(128)} %octs_hbm.1, s32[16]{0:T(128)} %pars_hbm.1, s32[16,32]{1,0:T(8,128)} %bitcast.7, s32[16,32]{1,0:T(8,128)} %bitcast.8, bf16[128,128]{1,0:T(8,128)(2,1)} %bitcast.6, bf16[16,8,2,128,128]{4,3,2,1,0:T(8,128)(2,1)} %near_hbm.1, ...), custom_call_target="tpu_custom_call" | custom-call | tf_op jit(solution)/shard_map/pallas_call | solution.py:398
  39.0 0.6 %copy.14 = f32[16,2,4,128]{3,2,1,0:T(4,128)} copy(f32[16,2,4,128]{3,2,1,0:T(4,128)S(1)} %bitcast.5) | data formatting | bytes 131072

commit v7 on v5

--- a/solution.py
+++ b/solution.py
@@ -227,10 +227,6 @@
             gathers[nz + t].wait()
 
         ids = gbuf[:, pl.ds(blk, boxes), :].reshape(slots, 128).astype(f32)
-        lane = lax.broadcasted_iota(jnp.int32, (slots, 128), 1).astype(f32)
-        spread = jnp.concatenate(
-            [jnp.where(ids == lane + 128.0 * h, 1.0, 0.0) for h in range(slots // 128)], axis=1
-        ).astype(bf16)
         ids_t = ids.T
         row = lax.broadcasted_iota(jnp.int32, (128, slots), 0).astype(f32)
         gather_m = jnp.concatenate(
@@ -277,6 +273,10 @@
                     parf[pl.ds(block * pb + 4 * c + r, parents, stride=8), :] = src(r, c).astype(f32)
             parw[pl.ds(block * parents, parents)] = parf[pl.ds(block * pb, pb), :].reshape(parents, 8, 128)
 
+        lane = lax.broadcasted_iota(jnp.int32, (slots, 128), 1).astype(f32)
+        spread = jnp.concatenate(
+            [jnp.where(ids == lane + 128.0 * h, 1.0, 0.0) for h in range(slots // 128)], axis=1
+        ).astype(bf16)
         keep(1, lambda r, c: parb[r, c])
         for side in range(2):
             halos[side].wait()

time: 39.7 us -> 39.7 us (level)
  no operation moved by 1% of the time
where the time goes in v7:
time: 39.7 us; the launch traced here: 39.6 us
  Pallas kernels  39 us (98%)
  local copies, waits for them, and re-layouts  0.63 us (2%)
    pallas_call x1, Pallas kernels, on_device(): pl.pallas_call(make_kernel(nbox, nsamp, boxes, parents, neighbours.shape[...  39 us

profile of v7, /device:TPU:2, one launch (start us, length us, event | category | flops | bytes accessed | tf_op | source)
XLA Modules:
  0.0 39.6 jit_solution(66113703549290587)
XLA Ops:
  0.0 39.0 %shard_map.118 = f32[128,128]{1,0:T(8,128)S(1)} custom-call(s32[8,16]{1,0:T(8,128)} %bitcast.9, s32[16]{0:T(128)} %octs_hbm.1, s32[16]{0:T(128)} %pars_hbm.1, s32[16,32]{1,0:T(8,128)} %bitcast.7, s32[16,32]{1,0:T(8,128)} %bitcast.8, bf16[128,128]{1,0:T(8,128)(2,1)} %bitcast.6, bf16[16,8,2,128,128]{4,3,2,1,0:T(8,128)(2,1)} %near_hbm.1, ...), custom_call_target="tpu_custom_call" | custom-call | tf_op jit(solution)/shard_map/pallas_call | solution.py:400
  39.0 0.6 %copy.14 = f32[16,2,4,128]{3,2,1,0:T(4,128)} copy(f32[16,2,4,128]{3,2,1,0:T(4,128)S(1)} %bitcast.5) | data formatting | bytes 131072
